TPU v7x, 32 devices: a whole 2x2x4 slice. The times are simulated.
32 devices in a mesh: freq: 2 (over x), facet: 16 (over z, y, core).
Axes of the slice: x: 2, y: 2, z: 4, core: 2. Of those that a mesh axis runs over, the one named last changes fastest.
Arguments:
- model_image: float32 [128, 2048], P('facet'), may hold values from -6 to 6
- visibilities: float32 [2, 8192], P(None, ('freq', 'facet')), may hold values from -6 to 6
- kernel_u: float32 [16, 8192], P(None, ('freq', 'facet')), may hold values from -1.5 to 1.5
- kernel_v: float32 [16, 8192], P(None, ('freq', 'facet')), may hold values from -1.5 to 1.5
- owners: int32 [8192, 1], P(('freq', 'facet')), may hold values from 0 to 15; in each aligned block of 256 rows (0 to 255, 256 to 511, ...) at most 64 rows name the same one
- offsets: int32 [2, 8192], P(None, ('freq', 'facet')), may hold values from 0 to 48
- corners: int32 [2, 16, 2], P('freq'), may hold values from -8192 to 8128
Outputs:
- model_out: float32 [128, 2048], P('facet')
- residual_rows: float32 [2, 8192], P(None, ('freq', 'facet'))
Inputs may be any that keep to these rules, and one draw needn't show every extreme that they name: `owners`: within each device's 256 rows, at most 64 rows name one owner, a bound that some block reaches of them.
All inputs are finite; a program needn't handle non-finite values.
Results may differ from a plain program's by a relative error of at most 0.0045.
Values sent between devices are 32-bit elements; how exact they have to be, the bound alone decides.
No kernel may reach another device: no remote copies, remote signals or barrier semaphores. Data moves between devices by JAX's collectives and lax.ppermute only.
A program may use at most 64 MiB of HBM per device.

v0:
```python
import math
import jax
import jax.numpy as jnp
from jax import lax
from jax.sharding import PartitionSpec as P

GRID = 16384
FACET = 2048
FROWS = 8
SUB = 64
SUPPORT = 16
CYCLES = 2
exact_products = lax.Precision.HIGHEST
GAIN_STEP = 0.5


def phase_pair(freq_index, position):
    angle_value = jnp.mod(freq_index * position, GRID).astype(jnp.float32) * (2.0 * math.pi / GRID)
    return (jnp.cos(angle_value), jnp.sin(angle_value))


def column_table():
    columns = jnp.arange(FACET, dtype=jnp.int32)
    frequency = jnp.arange(SUB, dtype=jnp.int32)
    cos_t, sin_t = phase_pair(frequency[None, :], columns[:, None])
    return jnp.concatenate([cos_t, sin_t], axis=1)


def make_back(col_table):
    cos_t = col_table[:, :SUB].T
    sin_t = col_table[:, SUB:].T
    upper = jnp.concatenate([cos_t, sin_t], axis=1)
    lower = jnp.concatenate([-sin_t, cos_t], axis=1)
    return jnp.concatenate([upper, lower], axis=0)


def forward_part(images, facet_ids, u_start, v_start, col_table):
    amount = images.shape[0]
    columns = jnp.arange(FACET, dtype=jnp.int32)
    cos_u, sin_u = phase_pair(u_start, columns)
    real_mod = (images * cos_u).reshape(amount * FROWS, FACET).astype(jnp.bfloat16)
    imag_mod = (-images * sin_u).reshape(amount * FROWS, FACET).astype(jnp.bfloat16)
    table_half = col_table.astype(jnp.bfloat16)
    real_prod = jnp.dot(real_mod, table_half, preferred_element_type=jnp.float32).reshape(
        amount, FROWS, 2 * SUB
    )
    imag_prod = jnp.dot(imag_mod, table_half, preferred_element_type=jnp.float32).reshape(
        amount, FROWS, 2 * SUB
    )
    col_re = real_prod[..., :SUB] + imag_prod[..., SUB:]
    col_im = imag_prod[..., :SUB] - real_prod[..., SUB:]
    frequency = jnp.arange(SUB, dtype=jnp.int32)
    x_start = facet_ids % (GRID // FACET) * FACET - GRID // 2
    cos_x, sin_x = phase_pair(u_start + frequency[None, :], x_start[:, None])
    shift_re = col_re * cos_x[:, None, :] + col_im * sin_x[:, None, :]
    shift_im = col_im * cos_x[:, None, :] - col_re * sin_x[:, None, :]
    y_pos = (facet_ids // (GRID // FACET) * FACET - GRID // 2)[:, None] + jnp.arange(
        FROWS, dtype=jnp.int32
    )[None, :]
    cosine_vertical, sine_vertical = phase_pair(v_start + frequency[:, None, None], y_pos[None])
    grid_re = jnp.einsum(
        "bfr,fra->ba", cosine_vertical, shift_re, precision=exact_products
    ) + jnp.einsum("bfr,fra->ba", sine_vertical, shift_im, precision=exact_products)
    grid_im = jnp.einsum(
        "bfr,fra->ba", cosine_vertical, shift_im, precision=exact_products
    ) - jnp.einsum("bfr,fra->ba", sine_vertical, shift_re, precision=exact_products)
    return jnp.stack([grid_re, grid_im], axis=1)


def forward_sum(images, facet_ids, u_start, v_start, col_table):
    amount = images.shape[0]
    blocking = math.gcd(amount, 8)

    def forward_accumulate(running, pieces):
        return (running + forward_part(pieces[0], pieces[1], u_start, v_start, col_table), None)

    sectioned = images.reshape(amount // blocking, blocking, FROWS, FACET)
    sectioned_ids = facet_ids.reshape(amount // blocking, blocking)
    running, unused = lax.scan(
        forward_accumulate, jnp.zeros((SUB, 2, SUB), jnp.float32), (sectioned, sectioned_ids)
    )
    return running


def adjoint_part(blocks, u_starts, v_starts, facet_here, back_table):
    amount = blocks.shape[0]
    frequency = jnp.arange(SUB, dtype=jnp.int32)
    y_pos = facet_here // (GRID // FACET) * FACET - GRID // 2 + jnp.arange(FROWS, dtype=jnp.int32)
    cosine_vertical, sine_vertical = phase_pair(
        v_starts[:, None, None] + frequency[None, :, None], y_pos[None, None, :]
    )
    kernel_real = blocks[:, :, 0, :]
    kernel_imaginary = blocks[:, :, 1, :]
    row_real = jnp.einsum(
        "gil,gik->glk", cosine_vertical, kernel_real, precision=exact_products
    ) - jnp.einsum("gil,gik->glk", sine_vertical, kernel_imaginary, precision=exact_products)
    row_imaginary = jnp.einsum(
        "gil,gik->glk", cosine_vertical, kernel_imaginary, precision=exact_products
    ) + jnp.einsum("gil,gik->glk", sine_vertical, kernel_real, precision=exact_products)
    x_start = facet_here % (GRID // FACET) * FACET - GRID // 2
    cos_x, sin_x = phase_pair(u_starts[:, None] + frequency[None, :], x_start)
    shift_re = row_real * cos_x[:, None, :] - row_imaginary * sin_x[:, None, :]
    shift_im = row_imaginary * cos_x[:, None, :] + row_real * sin_x[:, None, :]
    joined = (
        jnp.concatenate([shift_re, shift_im], axis=2)
        .reshape(amount * FROWS, 2 * SUB)
        .astype(jnp.bfloat16)
    )
    both = jnp.dot(
        joined, back_table.astype(jnp.bfloat16), preferred_element_type=jnp.float32
    ).reshape(amount, FROWS, 2 * FACET)
    columns = jnp.arange(FACET, dtype=jnp.int32)
    cos_u, sin_u = phase_pair(u_starts[:, None], columns[None, :])
    return jnp.sum(
        both[..., :FACET] * cos_u[:, None, :] - both[..., FACET:] * sin_u[:, None, :], axis=0
    )


def adjoint_sum(blocks, corner_list, facet_here, back_table):
    amount = blocks.shape[0]
    blocking = math.gcd(amount, 8)

    def adjoint_accumulate(running, pieces):
        return (
            running
            + adjoint_part(pieces[0], pieces[1][:, 0], pieces[1][:, 1], facet_here, back_table),
            None,
        )

    sectioned = blocks.reshape(amount // blocking, blocking, SUB, 2, SUB)
    starts = corner_list.reshape(amount // blocking, blocking, 2)
    running, unused = lax.scan(
        adjoint_accumulate, jnp.zeros((FROWS, FACET), jnp.float32), (sectioned, starts)
    )
    return running


def slot_positions(owner_ids, capacity, owner_count):
    owner_hits = (owner_ids[:, None] == jnp.arange(owner_count, dtype=jnp.int32)[None, :]).astype(
        jnp.int32
    )
    before = jnp.cumsum(owner_hits, axis=0) - owner_hits
    return owner_ids * capacity + jnp.sum(before * owner_hits, axis=1)


def place_kernel(kernel, offset_row):
    row_ids = jnp.arange(SUB, dtype=jnp.int32)[:, None]
    placed = jnp.zeros((SUB, kernel.shape[1]), jnp.float32)
    for kernel_tap in range(SUPPORT):
        placed = placed + jnp.where(
            row_ids == offset_row[None, :] + kernel_tap, kernel[kernel_tap][None, :], 0.0
        )
    return placed


def predict_rows(grid_block, kern_u, kern_v):
    partial_rows = jnp.einsum("bpa,ar->bpr", grid_block, kern_u, precision=exact_products)
    return jnp.sum(kern_v[:, None, :] * partial_rows, axis=0)


def grid_rows(residual, kern_u, kern_v):
    return jnp.einsum(
        "br,par->bpa", kern_v, residual[:, None, :] * kern_u[None], precision=exact_products
    )


def on_device(model_image, visibilities, kernel_u, kernel_v, owners, offsets, corners):
    facet_count = lax.axis_size("facet")
    facet_here = lax.axis_index("facet")
    device_rows = owners.shape[0]
    capacity = 4 * device_rows // facet_count
    scale = 1.0 / math.sqrt(facet_count * FROWS * FACET)
    slot_index = slot_positions(owners[:, 0], capacity, facet_count)
    payload = jnp.concatenate(
        [visibilities, kernel_u, kernel_v, offsets.astype(jnp.float32)], axis=0
    )
    feature_rows = payload.shape[0]
    send_buffer = (
        jnp.zeros((feature_rows, facet_count * capacity), jnp.float32)
        .at[:, slot_index]
        .set(payload)
    )
    send_buffer = send_buffer.reshape(feature_rows, facet_count, capacity)
    arrived = lax.all_to_all(send_buffer, "facet", split_axis=1, concat_axis=1, tiled=True).reshape(
        feature_rows, facet_count * capacity
    )
    observed = arrived[0:2]
    kern_u = place_kernel(arrived[2 : 2 + SUPPORT], arrived[2 + 2 * SUPPORT].astype(jnp.int32))
    kern_v = place_kernel(
        arrived[2 + SUPPORT : 2 + 2 * SUPPORT], arrived[3 + 2 * SUPPORT].astype(jnp.int32)
    )
    corner_list = corners[0]
    own_corner = corner_list[facet_here]
    col_table = column_table()
    back_table = make_back(col_table)
    current = model_image
    residual = observed
    for major_cycle in range(CYCLES):
        gathered = lax.all_gather(current, "facet", axis=0, tiled=True)
        amount = gathered.shape[0] // FROWS
        facet_ids = jnp.arange(amount, dtype=jnp.int32)
        summed = forward_sum(
            gathered.reshape(amount, FROWS, FACET),
            facet_ids,
            own_corner[0],
            own_corner[1],
            col_table,
        )
        grid_block = scale * summed
        residual = observed - predict_rows(grid_block, kern_u, kern_v)
        gridded = grid_rows(residual, kern_u, kern_v)
        add_gathered = lax.all_gather(gridded, "facet", axis=0, tiled=True)
        add_amount = add_gathered.shape[0] // SUB
        dirty_image = scale * adjoint_sum(
            add_gathered.reshape(add_amount, SUB, 2, SUB), corner_list, facet_here, back_table
        )
        current = current + GAIN_STEP * lax.psum(dirty_image, "freq")
    returned = lax.all_to_all(
        residual.reshape(2, facet_count, capacity), "facet", split_axis=1, concat_axis=1, tiled=True
    )
    returned = returned.reshape(2, facet_count * capacity)
    return (current, returned[:, slot_index])


def solution(mesh):
    return jax.shard_map(
        on_device,
        mesh=mesh,
        in_specs=(
            P("facet", None),
            P(None, ("freq", "facet")),
            P(None, ("freq", "facet")),
            P(None, ("freq", "facet")),
            P(("freq", "facet"), None),
            P(None, ("freq", "facet")),
            P("freq", None, None),
        ),
        out_specs=(P("facet", None), P(None, ("freq", "facet"))),
        check_vma=False,
    )
```

profile of v0, /device:TPU:0, one launch (start us, length us, event | category | flops | bytes accessed | tf_op | source)
XLA Modules:
  0.0 240.4 jit_solution(4313704084468116243)
XLA Ops:
  11.6 1.3 scatter_custom_fusion
  14.1 7.4 %all-to-all-start = ((f32[16,1,2304]{2,1,0:T(1,128)}), f32[16,1,2304]{2,1,0:T(1,128)S(1)}, u32[]{:S(2)}, u32[]{:S(2)}) async-start(f32[16,1,2304]{2,1,0:T(1,128)} %reshape.2303), calls=%async_computation | async-start | bytes 294912 | tf_op jit(solution)/shard_map/all_to_all | solution.py:184
  22.3 2.2 negate_convert_fusion
  24.4 2.0 fusion.234
  27.1 4.4 %sine_convert_fusion = (bf16[2048,64]{1,0:T(8,128)(2,1)S(1)}, bf16[2048,64]{1,0:T(8,128)(2,1)S(1)}) fusion(), kind=kLoop, calls=%fused_computation.325 | loop fusion | flops 2097152 | bytes 524288 | tf_op jit(solution)/shard_map/convert.11
  38.1 25.6 %all-gather.3.cloned.1.call-done = f32[128,2048]{1,0:T(8,128)} async-done(((f32[8,2048]{1,0:T(8,128)}), f32[128,2048]{1,0:T(8,128)}) %all-gather.3.cloned.1.call-update) | async-done | bytes 1048592 | tf_op jit(solution)/shard_map/all_gather | solution.py:199
  63.7 11.2 %while.58 = (s32[]{:T(128)}, f32[64,2,64]{2,0,1:T(8,128)S(1)}, s32[]{:T(128)}, s32[2,8]{1,0:T(2,128)S(1)}, f32[2,8,8,2048]{3,2,1,0:T(8,128)}, /*index=5*/s32[]{:...) while((s32[]{:T(128)}, f32[64,2,64]{2,0,1:T(8,128)S(1)}, s32[]{:T(128)}, ...), condition=%wide.region_5.6_spmd.clone, body=%wide.region_4.5_spmd.clone.sunk | while | flops 80678272 | bytes 6762359 | solution.py:79
  64.5 1.3 fusion.336
  70.1 1.3 fusion.336
  71.7 1.2 iota_add_fusion.18
  76.4 22.5 %all_gather.13 = f32[1024,2,64]{2,0,1:T(8,128)S(1)} all-gather(f32[64,2,64]{2,0,1:T(8,128)S(1)} %fusion.225), channel_id=1, replica_groups=mesh['freq'=2,'facet'=16] {'facet'}, dimensions={0}, use_global_device_ids=true | all-gather | bytes 557056 | tf_op jit(solution)/shard_map/all_gather | solution.py:212
  98.9 6.5 %while.59 = (s32[]{:T(128)}, f32[8,2048]{1,0:T(8,128)S(1)}, s32[2,8,2]{1,2,0:T(2,128)S(1)}, s32[]{:T(128)}, f32[2,8,64,2,64]{4,2,1,0,3:T(8,128)S(1)}, /*index=5*...) while((s32[]{:T(128)}, f32[8,2048]{1,0:T(8,128)S(1)}, s32[2,8,2]{1,2,0:T(2,128)S(1)}, ...), condition=%wide.region_9.10_spmd.clone, body=%wide.region_7.9_spmd.clone.sunk | while | flops 80773128 | bytes 5456375 | solution.py:132
  106.1 18.3 %all-reduce.3.cloned.1.call-done = f32[8,2048]{1,0:T(8,128)} async-done(((f32[8,2048]{1,0:T(8,128)}), f32[8,2048]{1,0:T(8,128)}) %all-reduce.3.cloned.1.call-update) | async-done | bytes 65552 | tf_op jit(solution)/shard_map/psum | solution.py:217
  124.4 1.5 multiply_add_fusion.5
  125.9 39.1 %all-gather.5.cloned.1.call-done = f32[128,2048]{1,0:T(8,128)} async-done(((f32[8,2048]{1,0:T(8,128)}), f32[128,2048]{1,0:T(8,128)}) %all-gather.5.cloned.1.call-update) | async-done | bytes 1048592 | tf_op jit(solution)/shard_map/all_gather | solution.py:199
  165.0 11.2 %while.60 = (s32[]{:T(128)}, f32[64,2,64]{2,0,1:T(8,128)S(1)}, s32[]{:T(128)}, s32[2,8]{1,0:T(2,128)S(1)}, f32[2,8,8,2048]{3,2,1,0:T(8,128)}, /*index=5*/s32[]{:...) while((s32[]{:T(128)}, f32[64,2,64]{2,0,1:T(8,128)S(1)}, s32[]{:T(128)}, ...), condition=%wide.region_12.13_spmd.clone, body=%wide.region_11.12_spmd.clone.sunk | while | flops 80678272 | bytes 6762359 | solution.py:79
  165.8 1.3 fusion.366
  171.4 1.3 fusion.366
  173.0 1.2 iota_add_fusion.22
  177.7 3.7 %all-to-all-start.1 = ((f32[16,1,128]{2,1,0:T(1,128)}), f32[16,1,128]{2,1,0:T(1,128)S(1)}, u32[]{:S(2)}, u32[]{:S(2)}) async-start(f32[16,1,128]{2,1,0:T(1,128)} %reshape.2305), calls=%async_computation.1 | async-start | bytes 16384 | tf_op jit(solution)/shard_map/all_to_all | solution.py:218
  182.3 24.6 %all_gather.15 = f32[1024,2,64]{2,0,1:T(8,128)S(1)} all-gather(f32[64,2,64]{2,0,1:T(8,128)S(1)} %fusion.221), channel_id=1, replica_groups=mesh['freq'=2,'facet'=16] {'facet'}, dimensions={0}, use_global_device_ids=true | all-gather | bytes 557056 | tf_op jit(solution)/shard_map/all_gather | solution.py:212
  206.9 6.5 %while.61 = (s32[]{:T(128)}, f32[8,2048]{1,0:T(8,128)S(1)}, s32[2,8,2]{1,2,0:T(2,128)S(1)}, s32[]{:T(128)}, f32[2,8,64,2,64]{4,2,1,0,3:T(8,128)S(1)}, /*index=5*...) while((s32[]{:T(128)}, f32[8,2048]{1,0:T(8,128)S(1)}, ...), condition=%wide.region_16.17_spmd.clone, body=%wide.region_14.16_spmd.clone.sunk | while | flops 80773128 | bytes 5456375 | solution.py:132
  216.5 15.9 %all-reduce.5.cloned.1.call-done = f32[8,2048]{1,0:T(8,128)} async-done(((f32[8,2048]{1,0:T(8,128)}), f32[8,2048]{1,0:T(8,128)}) %all-reduce.5.cloned.1.call-update) | async-done | bytes 65552 | tf_op jit(solution)/shard_map/psum | solution.py:217
  232.4 1.5 multiply_add_fusion.4
  (218 shorter events, 48.3 us)
Async XLA Ops:
  12.9 13.5 %copy-start.4 = (s32[1,16,2]{1,2,0:T(2,128)S(1)}, s32[1,16,2]{1,2,0:T(2,128)}, u32[]{:S(2)}) copy-start(s32[1,16,2]{1,2,0:T(2,128)} %param.21) | copy-start | bytes 388
  14.1 17.9 %all-to-all-start = ((f32[16,1,2304]{2,1,0:T(1,128)}), f32[16,1,2304]{2,1,0:T(1,128)S(1)}, u32[]{:S(2)}, u32[]{:S(2)}) async-start(f32[16,1,2304]{2,1,0:T(1,128)} %reshape.2303), calls=%async_computation | async-start | bytes 294912 | tf_op jit(solution)/shard_map/all_to_all | solution.py:184
  21.5 42.2 %all-gather.3.cloned.1.call-start = ((), (), s32[]{:S(2)}) async-start(), calls=%async_computation.2 | async-start | bytes 1114112 | tf_op jit(solution)/shard_map/all_gather | solution.py:199
  22.2 102.2 %all-reduce.3.cloned.1.call-start = ((), (), s32[]{:S(2)}) async-start(), calls=%async_computation.3 | async-start | bytes 131072 | tf_op jit(solution)/shard_map/psum | solution.py:217
  63.7 2.1 copy-start
  69.3 2.1 copy-start
  98.9 25.5 %copy-start.3 = (f32[8,2048]{1,0:T(8,128)S(1)}, f32[8,2048]{1,0:T(8,128)}, u32[]{:S(2)}) copy-start(f32[8,2048]{1,0:T(8,128)} %param.15) | copy-start | bytes 196612
  106.1 59.0 %all-gather.5.cloned.1.call-start = ((), (), s32[]{:S(2)}) async-start(), calls=%async_computation.4 | async-start | bytes 1114112 | tf_op jit(solution)/shard_map/all_gather | solution.py:199
  165.0 2.1 copy-start.1
  170.6 2.1 copy-start.1
  177.7 36.4 %all-to-all-start.1 = ((f32[16,1,128]{2,1,0:T(1,128)}), f32[16,1,128]{2,1,0:T(1,128)S(1)}, u32[]{:S(2)}, u32[]{:S(2)}) async-start(f32[16,1,128]{2,1,0:T(1,128)} %reshape.2305), calls=%async_computation.1 | async-start | bytes 16384 | tf_op jit(solution)/shard_map/all_to_all | solution.py:218
  181.3 51.0 %all-reduce.5.cloned.1.call-start = ((), (), s32[]{:S(2)}) async-start(), calls=%async_computation.5 | async-start | bytes 131072 | tf_op jit(solution)/shard_map/psum | solution.py:217
  206.9 25.5 %copy-start.2 = (f32[8,2048]{1,0:T(8,128)S(1)}, f32[8,2048]{1,0:T(8,128)}, u32[]{:S(2)}) copy-start(f32[8,2048]{1,0:T(8,128)} %multiply_add_fusion.5) | copy-start | bytes 196612
Sparse Core Ops, SparseCore 0:
  24.4 39.2 all-gather.2
  106.2 18.1 all-reduce.2
  127.1 37.8 all-gather.4
  214.2 18.1 all-reduce.4
where the time goes:
time: 241 us; the launch traced here: 240 us
  waiting for transfers between devices  99.6 us (41%)
  blocking collectives  47.1 us (20%)
  other arithmetic  32.1 us (13%)
  matrix products  25.6 us (11%)
  between operations  14.1 us (6%)
  starting transfers between devices  11.3 us (5%)
  local copies, waits for them, and re-layouts  10 us (4%)
    all_gather x2, waiting for transfers between devices, on_device(): gathered = lax.all_gather(current, 'facet', axis=0, tiled=True)  64.7 us
    all_gather x2, blocking collectives, on_device(): add_gathered = lax.all_gather(gridded, 'facet', axis=0, tiled=True)  47.1 us
    psum x2, waiting for transfers between devices, on_device(): current = current + GAIN_STEP * lax.psum(dirty_image, 'freq')  34.2 us
    another operation x5, other arithmetic  9.08 us
    all_to_all x1, starting transfers between devices, on_device(): lax.all_to_all(send_buffer, 'facet', split_axis=1, concat_axis=1, tiled=T...  7.41 us
    dot_general x4, matrix products, forward_part(): jnp.dot(imag_mod, table_half, preferred_element_type=jnp.float32)  5.08 us
  transfers between devices with their start and end apart: 6, of which 4 were waited for; matrix products, arithmetic and copies ran while one was open for 11% of the time, Pallas kernels for 0%

commit v1 on v0

--- a/solution.py
+++ b/solution.py
@@ -12,6 +12,12 @@
 CYCLES = 2
 exact_products = lax.Precision.HIGHEST
 GAIN_STEP = 0.5
+
+
+def summed_here(value, axis):
+    shards = lax.all_gather(value, axis, axis=0, tiled=False)
+    total = shards.sum(axis=0)
+    return total
 
 
 def phase_pair(freq_index, position):
@@ -214,7 +220,7 @@
         dirty_image = scale * adjoint_sum(
             add_gathered.reshape(add_amount, SUB, 2, SUB), corner_list, facet_here, back_table
         )
-        current = current + GAIN_STEP * lax.psum(dirty_image, "freq")
+        current = current + GAIN_STEP * summed_here(dirty_image, "freq")
     returned = lax.all_to_all(
         residual.reshape(2, facet_count, capacity), "facet", split_axis=1, concat_axis=1, tiled=True
     )

time: 241 us -> 210 us (0.87)
  waiting for transfers between devices: 99.6 us -> 61.5 us
  blocking collectives: 47.1 us -> 57.2 us
  other arithmetic: 32.1 us -> 29.1 us
    psum x2 -> x0, waiting for transfers between devices: 34.2 us -> none  [on_device(): current = current + GAIN_STEP * lax.psum(dirty_image, 'freq')]
    all_gather x0 -> x2, blocking collectives: none -> 10 us  [summed_here(): shards = lax.all_gather(value, axis, axis=0, tiled=False)]
    all_gather x2, waiting for transfers between devices: 64.7 us -> 60.8 us  [on_device(): gathered = lax.all_gather(current, 'facet', axis=0, tiled=True)]
  transfers between devices with their start and end apart: 6 -> 4, of which waited for: 4 -> 2; matrix products, arithmetic and copies ran while one was open for 11% -> 11% of each run, Pallas kernels for 0% -> 0%
where the time goes in v1:
time: 210 us
  waiting for transfers between devices  61.5 us (29%)
  blocking collectives  57.2 us (27%)
  other arithmetic  29.1 us (14%)
  matrix products  25.5 us (12%)
  between operations  14.4 us (7%)
  starting transfers between devices  11.2 us (5%)
  local copies, waits for them, and re-layouts  10 us (5%)
    all_gather x2, waiting for transfers between devices, on_device(): gathered = lax.all_gather(current, 'facet', axis=0, tiled=True)  60.8 us
    all_gather x2, blocking collectives, on_device(): add_gathered = lax.all_gather(gridded, 'facet', axis=0, tiled=True)  47.1 us
    all_gather x2, blocking collectives, summed_here(): shards = lax.all_gather(value, axis, axis=0, tiled=False)  10 us
    another operation x5, other arithmetic  9.08 us
    all_to_all x1, starting transfers between devices, on_device(): lax.all_to_all(send_buffer, 'facet', split_axis=1, concat_axis=1, tiled=T...  7.41 us
    dot_general x4, matrix products, forward_part(): jnp.dot(imag_mod, table_half, preferred_element_type=jnp.float32)  5.06 us
    add x4, other arithmetic, forward_part(): cos_x, sin_x = phase_pair(u_start + frequency[None, :], x_start[:, None])  4.8 us
  transfers between devices with their start and end apart: 4, of which 2 were waited for; matrix products, arithmetic and copies ran while one was open for 11% of the time, Pallas kernels for 0%

profile of v1, /device:TPU:0, one launch (start us, length us, event | category | flops | bytes accessed | tf_op | source)
XLA Modules:
  0.0 209.6 jit_solution(17887064475293622601)
XLA Ops:
  11.6 1.3 scatter_custom_fusion
  14.1 7.4 %all-to-all-start = ((f32[16,1,2304]{2,1,0:T(1,128)}), f32[16,1,2304]{2,1,0:T(1,128)S(1)}, u32[]{:S(2)}, u32[]{:S(2)}) async-start(f32[16,1,2304]{2,1,0:T(1,128)} %reshape.2305), calls=%async_computation | async-start | bytes 294912 | tf_op jit(solution)/shard_map/all_to_all | solution.py:190
  22.3 2.2 %negate_convert_fusion = (bf16[64,2048]{1,0:T(8,128)(2,1)S(1)}, bf16[64,2048]{1,0:T(8,128)(2,1)S(1)}) fusion(), kind=kLoop, calls=%fused_computation.339 | loop fusion | flops 2228224 | bytes 524288 | tf_op jit(solution)/shard_map/convert.6
  24.4 2.0 fusion.234
  27.1 4.4 %sine_convert_fusion = (bf16[2048,64]{1,0:T(8,128)(2,1)S(1)}, bf16[2048,64]{1,0:T(8,128)(2,1)S(1)}) fusion(), kind=kLoop, calls=%fused_computation.325 | loop fusion | flops 2097152 | bytes 524288 | tf_op jit(solution)/shard_map/convert.11
  38.1 25.6 %all-gather.5.cloned.1.call-done = f32[128,2048]{1,0:T(8,128)} async-done(((f32[8,2048]{1,0:T(8,128)}), f32[128,2048]{1,0:T(8,128)}) %all-gather.5.cloned.1.call-update) | async-done | bytes 1048592 | tf_op jit(solution)/shard_map/all_gather | solution.py:205
  63.7 11.2 %while.58 = (s32[]{:T(128)}, f32[64,2,64]{2,0,1:T(8,128)S(1)}, s32[]{:T(128)}, s32[2,8]{1,0:T(2,128)S(1)}, f32[2,8,8,2048]{3,2,1,0:T(8,128)}, /*index=5*/s32[]{:...) while((s32[]{:T(128)}, f32[64,2,64]{2,0,1:T(8,128)S(1)}, s32[]{:T(128)}, ...), condition=%wide.region_5.6_spmd.clone, body=%wide.region_4.5_spmd.clone.sunk | while | flops 80678272 | bytes 6762359 | solution.py:85
  64.5 1.3 fusion.336
  66.0 1.2 iota_add_fusion.18
  70.1 1.3 fusion.336
  71.7 1.2 iota_add_fusion.18
  76.4 22.5 %all_gather.25 = f32[1024,2,64]{2,0,1:T(8,128)S(1)} all-gather(f32[64,2,64]{2,0,1:T(8,128)S(1)} %fusion.225), channel_id=1, replica_groups=mesh['freq'=2,'facet'=16] {'facet'}, dimensions={0}, use_global_device_ids=true | all-gather | bytes 557056 | tf_op jit(solution)/shard_map/all_gather | solution.py:218
  98.9 6.5 %while.59 = (s32[]{:T(128)}, f32[8,2048]{1,0:T(8,128)S(1)}, s32[2,8,2]{1,2,0:T(2,128)S(1)}, s32[]{:T(128)}, f32[2,8,64,2,64]{4,2,1,0,3:T(8,128)S(1)}, /*index=5*...) while((s32[]{:T(128)}, f32[8,2048]{1,0:T(8,128)S(1)}, s32[2,8,2]{1,2,0:T(2,128)S(1)}, ...), condition=%wide.region_9.10_spmd.clone, body=%wide.region_7.9_spmd.clone.sunk | while | flops 80773128 | bytes 5456375 | solution.py:138
  105.4 5.0 %all-gather = f32[16,2048]{1,0:T(8,128)S(1)} all-gather(f32[8,2048]{1,0:T(8,128)S(1)} %broadcast_multiply_fusion.1), channel_id=2, replica_groups=mesh['freq'=2,'facet'=16] {'freq'}, dimensions={0}, use_global_device_ids=true | all-gather | bytes 196608 | tf_op jit(solution)/shard_map/all_gather | solution.py:18
  111.1 35.2 %all-gather.7.cloned.1.call-done = f32[128,2048]{1,0:T(8,128)} async-done(((f32[8,2048]{1,0:T(8,128)}), f32[128,2048]{1,0:T(8,128)}) %all-gather.7.cloned.1.call-update) | async-done | bytes 1048592 | tf_op jit(solution)/shard_map/all_gather | solution.py:205
  146.3 11.2 %while.60 = (s32[]{:T(128)}, f32[64,2,64]{2,0,1:T(8,128)S(1)}, s32[]{:T(128)}, s32[2,8]{1,0:T(2,128)S(1)}, f32[2,8,8,2048]{3,2,1,0:T(8,128)}, /*index=5*/s32[]{:...) while((s32[]{:T(128)}, f32[64,2,64]{2,0,1:T(8,128)S(1)}, s32[]{:T(128)}, ...), condition=%wide.region_12.13_spmd.clone, body=%wide.region_11.12_spmd.clone.sunk | while | flops 80678272 | bytes 6762359 | solution.py:85
  147.1 1.3 fusion.366
  148.7 1.2 iota_add_fusion.22
  152.7 1.3 fusion.366
  154.3 1.2 iota_add_fusion.22
  159.0 3.7 %all-to-all-start.1 = ((f32[16,1,128]{2,1,0:T(1,128)}), f32[16,1,128]{2,1,0:T(1,128)S(1)}, u32[]{:S(2)}, u32[]{:S(2)}) async-start(f32[16,1,128]{2,1,0:T(1,128)} %reshape.2307), calls=%async_computation.1 | async-start | bytes 16384 | tf_op jit(solution)/shard_map/all_to_all | solution.py:224
  163.5 24.6 %all_gather.29 = f32[1024,2,64]{2,0,1:T(8,128)S(1)} all-gather(f32[64,2,64]{2,0,1:T(8,128)S(1)} %fusion.221), channel_id=1, replica_groups=mesh['freq'=2,'facet'=16] {'facet'}, dimensions={0}, use_global_device_ids=true | all-gather | bytes 557056 | tf_op jit(solution)/shard_map/all_gather | solution.py:218
  188.2 6.5 %while.61 = (s32[]{:T(128)}, f32[8,2048]{1,0:T(8,128)S(1)}, s32[2,8,2]{1,2,0:T(2,128)S(1)}, s32[]{:T(128)}, f32[2,8,64,2,64]{4,2,1,0,3:T(8,128)S(1)}, /*index=5*...) while((s32[]{:T(128)}, f32[8,2048]{1,0:T(8,128)S(1)}, ...), condition=%wide.region_16.17_spmd.clone, body=%wide.region_14.16_spmd.clone.sunk | while | flops 80773128 | bytes 5456375 | solution.py:138
  194.7 5.0 %all-gather.1 = f32[16,2048]{1,0:T(8,128)S(1)} all-gather(f32[8,2048]{1,0:T(8,128)S(1)} %broadcast_multiply_fusion), channel_id=3, replica_groups=mesh['freq'=2,'facet'=16] {'freq'}, dimensions={0}, use_global_device_ids=true | all-gather | bytes 196608 | tf_op jit(solution)/shard_map/all_gather | solution.py:18
  (216 shorter events, 45.8 us)
Async XLA Ops:
  12.9 13.5 %copy-start.4 = (s32[1,16,2]{1,2,0:T(2,128)S(1)}, s32[1,16,2]{1,2,0:T(2,128)}, u32[]{:S(2)}) copy-start(s32[1,16,2]{1,2,0:T(2,128)} %param.21) | copy-start | bytes 388
  14.1 17.9 %all-to-all-start = ((f32[16,1,2304]{2,1,0:T(1,128)}), f32[16,1,2304]{2,1,0:T(1,128)S(1)}, u32[]{:S(2)}, u32[]{:S(2)}) async-start(f32[16,1,2304]{2,1,0:T(1,128)} %reshape.2305), calls=%async_computation | async-start | bytes 294912 | tf_op jit(solution)/shard_map/all_to_all | solution.py:190
  21.5 42.2 %all-gather.5.cloned.1.call-start = ((), (), s32[]{:S(2)}) async-start(), calls=%async_computation.2 | async-start | bytes 1114112 | tf_op jit(solution)/shard_map/all_gather | solution.py:205
  22.2 124.1 %all-gather.7.cloned.1.call-start = ((), (), s32[]{:S(2)}) async-start(), calls=%async_computation.3 | async-start | bytes 1114112 | tf_op jit(solution)/shard_map/all_gather | solution.py:205
  63.7 2.1 copy-start
  69.3 2.1 copy-start
  98.9 11.5 %copy-start.3 = (f32[8,2048]{1,0:T(8,128)S(1)}, f32[8,2048]{1,0:T(8,128)}, u32[]{:S(2)}) copy-start(f32[8,2048]{1,0:T(8,128)} %param.15) | copy-start | bytes 196612
  146.3 2.1 copy-start.1
  152.0 2.1 copy-start.1
  159.0 41.4 %all-to-all-start.1 = ((f32[16,1,128]{2,1,0:T(1,128)}), f32[16,1,128]{2,1,0:T(1,128)S(1)}, u32[]{:S(2)}, u32[]{:S(2)}) async-start(f32[16,1,128]{2,1,0:T(1,128)} %reshape.2307), calls=%async_computation.1 | async-start | bytes 16384 | tf_op jit(solution)/shard_map/all_to_all | solution.py:224
  188.2 11.5 %copy-start.2 = (f32[8,2048]{1,0:T(8,128)S(1)}, f32[8,2048]{1,0:T(8,128)}, u32[]{:S(2)}) copy-start(f32[8,2048]{1,0:T(8,128)} %multiply_add_fusion.5) | copy-start | bytes 196612
Sparse Core Ops, SparseCore 0:
  24.4 39.2 all-gather.4
  111.2 35.0 all-gather.6
